TPU v7x, 32 devices: a whole 2x2x4 slice. The times are simulated.
32 devices in a mesh: comp: 4 (over y, core), tile: 8 (over z, x).
Axes of the slice: x: 2, y: 2, z: 4, core: 2. Of those that a mesh axis runs over, the one named last changes fastest.
Arguments:
- column_state: float32 [4, 8, 4, 16, 2048], P('comp', 'tile'), may hold values from -6 to 6
- mixing: float32 [2, 4, 16], replicated, may hold values from 0.02 to 0.24
- vertical: float32 [2, 16, 16], replicated, may hold values from -1.5 to 1.5
- flux_coef: float32 [2, 4], replicated, may hold values from 0.5 to 1.5
- atm_block: int32 [4, 8, 16], P('comp', 'tile'), may hold values from 0 to 15
- ocean_block: int32 [4, 8, 16], P('comp', 'tile'), may hold values from 0 to 15
- tile_offset: int32 [4, 8, 16], P('comp', 'tile'), may hold values from 0 to 6
- remap_weights: bfloat16 [4, 8, 16, 128, 128], P('comp', 'tile'), may hold values from 0 to 0.119628906
- ocean_mask: int32 [8, 2048], P('tile'), may hold values 0 or 1
Outputs:
- new_state: float32 [4, 8, 4, 16, 2048], P('comp', 'tile')
Inputs may be any that keep to these rules, and one draw needn't show every extreme that they name: `atm_block`: entries at comp index 3 are not read.
All inputs are finite; a program needn't handle non-finite values. No bound on the sum of `ocean_mask` on one device may be relied on, other than what follows from the above.
Results may differ from a plain program's by a relative error of at most 0.0003.
Values sent between devices are 32-bit elements; how exact they have to be, the bound alone decides.
No kernel may reach another device: no remote copies, remote signals or barrier semaphores. Data moves between devices by JAX's collectives and lax.ppermute only.
A program may use at most 64 MiB of HBM per device.

v0:
```python
import jax
import jax.numpy as jnp
from jax import lax
from jax.sharding import PartitionSpec as P

REACH = 3
SUB = 2


def extended(cells, sides, width):
    for axis, dim in sides:
        count = lax.axis_size(axis)
        head = lax.slice_in_dim(cells, 0, width, axis=dim)
        tail = lax.slice_in_dim(cells, cells.shape[dim] - width, cells.shape[dim], axis=dim)
        cells = jnp.concatenate(
            [
                lax.ppermute(tail, axis, [(i, (i + 1) % count) for i in range(count)]),
                cells,
                lax.ppermute(head, axis, [((i + 1) % count, i) for i in range(count)]),
            ],
            axis=dim,
        )
    return cells


def passed_along(value, axis, steps):
    count = lax.axis_size(axis)
    pairs = [(source, (source + steps) % count) for source in range(count)]
    return lax.ppermute(value, axis, pairs)


def local(
    column_state,
    mixing,
    vertical,
    flux_coef,
    atm_block,
    ocean_block,
    tile_offset,
    remap_weights,
    ocean_mask,
):
    fields = column_state[0, 0]
    cells = fields.shape[2]
    across = remap_weights.shape[3]
    ocean_cells = remap_weights.shape[4]
    oblocks = cells // ocean_cells
    spread = 2 * REACH + 1
    comp_index = lax.axis_index("comp")
    comp_count = lax.axis_size("comp")
    is_atmos = comp_index < comp_count - 1
    group = jnp.where(is_atmos, 0, 1).astype(jnp.int32)
    rates = lax.dynamic_index_in_dim(mixing, group, 0, keepdims=False)[:, :, None]
    operator = lax.dynamic_index_in_dim(vertical, group, 0, keepdims=False)
    for sweep in range(SUB):
        padded = extended(fields, (("tile", 2),), 1)
        fields = fields + rates * (padded[:, :, :-2] + padded[:, :, 2:] - 2.0 * fields)
    mixed = fields + jnp.einsum("lm,kmz->klz", operator, fields, precision=lax.Precision.HIGHEST)
    surface = jnp.tanh(flux_coef[0][:, None] * mixed[:, -1] + flux_coef[1][:, None] * mixed[:, -2])
    rounded = surface.astype(jnp.bfloat16)
    blocks = rounded.reshape(rounded.shape[0], cells // across, across)
    chosen = blocks[:, atm_block[0, 0], :]
    contrib = jnp.einsum(
        "knb,nbj->nkj", chosen, remap_weights[0, 0], preferred_element_type=jnp.float32
    )
    by_offset = (tile_offset[0, 0][:, None] == jnp.arange(spread, dtype=jnp.int32)[None, :]).astype(
        jnp.float32
    )
    by_block = (ocean_block[0, 0][:, None] == jnp.arange(oblocks, dtype=jnp.int32)[None, :]).astype(
        jnp.float32
    )
    buffers = jnp.einsum(
        "nd,no,nkj->dkoj", by_offset, by_block, contrib, precision=lax.Precision.HIGHEST
    )
    buffers = buffers.reshape(spread, rounded.shape[0], cells)
    buffers = jnp.where(is_atmos, buffers, 0.0)
    received = buffers[REACH]
    for offset in range(-REACH, REACH + 1):
        if offset != 0:
            received = received + passed_along(buffers[REACH + offset], "tile", offset)
    received = lax.psum(received, "comp")
    land = ocean_mask[0].astype(jnp.float32)
    atmosphere = mixed.at[:, -1].add(-0.5 * surface)
    ocean = mixed.at[:, 0].add(land[None, :] * received)
    result = jnp.where(is_atmos, atmosphere, ocean)
    return result[None, None]


def solution(mesh):
    placed = (
        P("comp", "tile", None, None, None),
        P(),
        P(),
        P(),
        P("comp", "tile", None),
        P("comp", "tile", None),
        P("comp", "tile", None),
        P("comp", "tile", None, None, None),
        P("tile", None),
    )
    return jax.shard_map(
        local,
        mesh=mesh,
        in_specs=placed,
        out_specs=P("comp", "tile", None, None, None),
        check_vma=False,
    )
```

profile of v0, /device:TPU:0, one launch (start us, length us, event | category | flops | bytes accessed | tf_op | source)
XLA Modules:
  0.0 47.1 jit_solution(6400851959491823201)
XLA Ops:
  0.0 0.0 copy-start
  0.0 1.4 %copy.46 = f32[1,1,4,16,2048]{4,2,3,1,0:T(4,128)S(1)} copy(f32[1,1,4,16,2048]{4,3,2,1,0:T(8,128)} %param.13) | data formatting | bytes 1048576 | tf_op args[0]
  1.4 0.1 fusion.36
  1.5 3.0 %collective-permute-start = (f32[4,16,1]{2,0,1:T(4,128)S(1)}, f32[4,16,1]{2,0,1:T(4,128)S(1)}, u32[]{:S(2)}, u32[]{:S(2)}) collective-permute-start(f32[4,16,1]{2,0,1:T(4,128)S(1)} %get-tuple-element.35), channel_id=1, source_target_pairs={{0,1},{1,2},{2,3},{3,4},{4,5},{5,6},{6,7},{7,0},{8,9},{9,10},{10,1... | collective-permute-start | bytes 776 | tf_op jit(solution)/shard_map/ppermute | solution.py:17
  4.5 3.1 %collective-permute-start.1 = (f32[4,16,1]{2,0,1:T(4,128)S(1)}, f32[4,16,1]{2,0,1:T(4,128)S(1)}, u32[]{:S(2)}, u32[]{:S(2)}) collective-permute-start(f32[4,16,1]{2,0,1:T(4,128)S(1)} %get-tuple-element.36), channel_id=1, source_target_pairs={{1,0},{2,1},{3,2},{4,3},{5,4},{6,5},{7,6},{0,7},{9,8},{10,9},{11,1... | collective-permute-start | bytes 776 | tf_op jit(solution)/shard_map/ppermute | solution.py:19
  7.6 0.0 copy-start.4
  7.6 0.7 %copy-done.4 = f32[2,4]{1,0:T(2,128)S(1)} copy-done((f32[2,4]{1,0:T(2,128)S(1)}, f32[2,4]{1,0:T(2,128)}, u32[]{:S(2)}) %copy-start.4) | copy-done | bytes 56
  8.3 0.0 copy-start.7
  8.3 0.6 %copy-done.7 = s32[1,1,16]{2,1,0:T(1,128)S(1)} copy-done((s32[1,1,16]{2,1,0:T(1,128)S(1)}, s32[1,1,16]{2,1,0:T(1,128)}, u32[]{:S(2)}) %copy-start.7) | copy-done | bytes 88
  9.0 0.0 copy-start.5
  9.0 0.7 %copy-done.5 = s32[1,1,16]{2,1,0:T(1,128)S(1)} copy-done((s32[1,1,16]{2,1,0:T(1,128)S(1)}, s32[1,1,16]{2,1,0:T(1,128)}, u32[]{:S(2)}) %copy-start.5) | copy-done | bytes 88
  9.6 0.7 %copy-done.6 = s32[1,1,16]{2,1,0:T(1,128)S(1)} copy-done((s32[1,1,16]{2,1,0:T(1,128)S(1)}, s32[1,1,16]{2,1,0:T(1,128)}, u32[]{:S(2)}) %copy-start.6) | copy-done | bytes 88
  10.3 0.7 %copy-done.3 = f32[2,4,16]{2,1,0:T(4,128)S(1)} copy-done((f32[2,4,16]{2,1,0:T(4,128)S(1)}, f32[2,4,16]{2,1,0:T(4,128)}, u32[]{:S(2)}) %copy-start.3) | copy-done | bytes 536
  11.0 0.1 copy.13
  11.1 0.0 collective-permute-done
  11.1 0.0 collective-permute-done.1
  11.1 0.6 %fusion.8 = f32[4,16,2048]{2,0,1:T(4,128)S(1)} fusion(f32[4,16,2048]{2,0,1:T(4,128)S(1)} %bitcast.114, f32[4,16,1]{2,0,1:T(4,128)S(1)} %collective-permute-done.1, f32[4,16,1]{2,0,1:T(4,128)S(1)} %collective-permute-done, f32[4,16]{0,1:T(8,128)S(1)} %copy.13), kind=kLoop, calls=%fused_computation.13 | loop fusion | flops 917504 | bytes 1049344 | tf_op jit(solution)/shard_map/add | solution.py:57
  11.7 0.1 fusion.35
  11.8 0.0 collective-permute-start.2
  11.8 4.7 %collective-permute-start.3 = (f32[4,16,1]{2,0,1:T(4,128)S(1)}, f32[4,16,1]{2,0,1:T(4,128)S(1)}, u32[]{:S(2)}, u32[]{:S(2)}) collective-permute-start(f32[4,16,1]{2,0,1:T(4,128)S(1)} %get-tuple-element.34), channel_id=1, source_target_pairs={{1,0},{2,1},{3,2},{4,3},{5,4},{6,5},{7,6},{0,7},{9,8},{10,9},{11,1... | collective-permute-start | bytes 776 | tf_op jit(solution)/shard_map/ppermute | solution.py:19
  16.5 1.9 %collective-permute-done.2 = f32[4,16,1]{2,0,1:T(4,128)S(1)} collective-permute-done((f32[4,16,1]{2,0,1:T(4,128)S(1)}, f32[4,16,1]{2,0,1:T(4,128)S(1)}, u32[]{:S(2)}, u32[]{:S(2)}) %collective-permute-start.2) | collective-permute-done | bytes 288 | tf_op jit(solution)/shard_map/ppermute | solution.py:17
  18.4 0.0 collective-permute-done.3
  18.4 0.6 %fusion.4 = f32[4,16,2048]{2,0,1:T(4,128)S(1)} fusion(f32[4,16,2048]{2,0,1:T(4,128)S(1)} %fusion.8, f32[4,16,1]{2,0,1:T(4,128)S(1)} %collective-permute-done.3, f32[4,16,1]{2,0,1:T(4,128)S(1)} %collective-permute-done.2, f32[4,16]{0,1:T(8,128)S(1)} %copy.13), kind=kLoop, calls=%fused_computation.7 | loop fusion | flops 917504 | bytes 1049344 | tf_op jit(solution)/shard_map/add | solution.py:57
  19.1 0.0 copy-done.2
  19.1 0.9 %fusion.11 = f32[4,2048,16]{1,2,0:T(8,128)S(1)} fusion(f32[4,16,2048]{2,0,1:T(4,128)S(1)} %fusion.4, f32[2,16,16]{2,1,0:T(8,128)S(1)} %copy-done.2, s32[]{:T(128)S(6)} %select_n.39), kind=kOutput, calls=%fused_computation.18 | convolution fusion | flops 25165824 | bytes 1056772 | tf_op jit(solution)/shard_map/lm,kmz->klz/dot_general | solution.py:58
  20.0 0.7 %bitcast_add_fusion = f32[4,16,2048]{2,0,1:T(4,128)S(1)} fusion(f32[4,2048,16]{1,2,0:T(8,128)S(1)} %fusion.11, f32[4,16,2048]{2,0,1:T(4,128)S(1)} %fusion.8, f32[4,16,1]{2,0,1:T(4,128)S(1)} %collective-permute-done.3, f32[4,16,1]{2,0,1:T(4,128)S(1)} %collective-permute-done.2, f32[4,16]{0,1:T(8,128)S(1)} %copy.13), kind=kLoop, calls=%fused_computation.17 | loop fusion | flops 1048576 | bytes 1573632 | tf_op jit(solution)/shard_map/add | solution.py:58
  20.7 0.1 fusion.22
  20.8 0.6 %gather_fusion = bf16[16,4,128]{2,1,0:T(4,128)(2,1)S(1)} fusion(bf16[4,16,128]{2,0,1:T(4,128)(2,1)S(1)} %copy.16, s32[1024]{0:T(1024)S(1)} %pad_clamp_fusion), kind=kCustom, calls=%fused_computation | custom fusion | bytes 32832 | tf_op jit(solution)/shard_map/gather | solution.py:62
  21.4 0.0 copy-done
  21.4 0.2 fusion.9
  21.6 0.3 fusion
  22.0 1.6 %collective-permute-start.4 = (f32[4,2048]{1,0:T(4,128)S(1)}, f32[4,2048]{1,0:T(4,128)S(1)}, u32[]{:S(2)}, u32[]{:S(2)}) collective-permute-start(f32[4,2048]{1,0:T(4,128)S(1)} %bitcast.117), channel_id=1, source_target_pairs={{0,5},{1,6},{2,7},{3,0},{4,1},{5,2},{6,3},{7,4},{8,13},{9,14},{10,... | collective-permute-start | bytes 98312 | tf_op jit(solution)/shard_map/ppermute | solution.py:29
  23.7 1.4 %collective-permute-start.5 = (f32[4,2048]{1,0:T(4,128)S(1)}, f32[4,2048]{1,0:T(4,128)S(1)}, u32[]{:S(2)}, u32[]{:S(2)}) collective-permute-start(f32[4,2048]{1,0:T(4,128)S(1)} %bitcast.115), channel_id=1, source_target_pairs={{0,6},{1,7},{2,0},{3,1},{4,2},{5,3},{6,4},{7,5},{8,14},{9,15},{10,... | collective-permute-start | bytes 98312 | tf_op jit(solution)/shard_map/ppermute | solution.py:29
  25.1 1.9 %collective-permute-start.6 = (f32[4,2048]{1,0:T(4,128)S(1)}, f32[4,2048]{1,0:T(4,128)S(1)}, u32[]{:S(2)}, u32[]{:S(2)}) collective-permute-start(f32[4,2048]{1,0:T(4,128)S(1)} %bitcast.116), channel_id=1, source_target_pairs={{0,7},{1,0},{2,1},{3,2},{4,3},{5,4},{6,5},{7,6},{8,15},{9,8},{10,9... | collective-permute-start | bytes 98312 | tf_op jit(solution)/shard_map/ppermute | solution.py:29
  27.0 0.6 %collective-permute-start.7 = (f32[4,2048]{1,0:T(4,128)S(1)}, f32[4,2048]{1,0:T(4,128)S(1)}, u32[]{:S(2)}, u32[]{:S(2)}) collective-permute-start(f32[4,2048]{1,0:T(4,128)S(1)} %bitcast.118), channel_id=1, source_target_pairs={{0,1},{1,2},{2,3},{3,4},{4,5},{5,6},{6,7},{7,0},{8,9},{9,10},{10,1... | collective-permute-start | bytes 98312 | tf_op jit(solution)/shard_map/ppermute | solution.py:29
  27.6 2.1 %collective-permute-start.8 = (f32[4,2048]{1,0:T(4,128)S(1)}, f32[4,2048]{1,0:T(4,128)S(1)}, u32[]{:S(2)}, u32[]{:S(2)}) collective-permute-start(f32[4,2048]{1,0:T(4,128)S(1)} %bitcast.119), channel_id=1, source_target_pairs={{0,2},{1,3},{2,4},{3,5},{4,6},{5,7},{6,0},{7,1},{8,10},{9,11},{10,... | collective-permute-start | bytes 98312 | tf_op jit(solution)/shard_map/ppermute | solution.py:29
  29.7 0.0 collective-permute-done.4
  29.7 1.5 %collective-permute-start.9 = (f32[4,2048]{1,0:T(4,128)S(1)}, f32[4,2048]{1,0:T(4,128)S(1)}, u32[]{:S(2)}, u32[]{:S(2)}) collective-permute-start(f32[4,2048]{1,0:T(4,128)S(1)} %bitcast.120), channel_id=1, source_target_pairs={{0,3},{1,4},{2,5},{3,6},{4,7},{5,0},{6,1},{7,2},{8,11},{9,12},{10,... | collective-permute-start | bytes 98312 | tf_op jit(solution)/shard_map/ppermute | solution.py:29
  31.2 0.0 copy-done.1
  31.3 0.0 collective-permute-done.5
  31.3 0.0 collective-permute-done.6
  31.3 2.3 %collective-permute-done.7 = f32[4,2048]{1,0:T(4,128)S(1)} collective-permute-done((f32[4,2048]{1,0:T(4,128)S(1)}, f32[4,2048]{1,0:T(4,128)S(1)}, u32[]{:S(2)}, u32[]{:S(2)}) %collective-permute-start.7) | collective-permute-done | bytes 32800 | tf_op jit(solution)/shard_map/ppermute | solution.py:29
  33.6 0.0 collective-permute-done.8
  33.6 1.8 %collective-permute-done.9 = f32[4,2048]{1,0:T(4,128)S(1)} collective-permute-done((f32[4,2048]{1,0:T(4,128)S(1)}, f32[4,2048]{1,0:T(4,128)S(1)}, u32[]{:S(2)}, u32[]{:S(2)}) %collective-permute-start.9) | collective-permute-done | bytes 32800 | tf_op jit(solution)/shard_map/ppermute | solution.py:29
  35.5 10.3 %psum.7 = f32[4,2048]{1,0:T(4,128)S(1)} all-reduce(f32[4,2048]{1,0:T(4,128)S(1)} %fusion.19), channel_id=1, replica_groups=mesh['comp'=4,'tile'=8] {'comp'}, use_global_device_ids=true, to_apply=%region_0.1 | all-reduce | flops 8192 | bytes 65536 | tf_op jit(solution)/shard_map/psum | solution.py:81
  45.8 0.1 add_dynamic-update-slice_fusion
  45.9 0.1 select_bitcast_fusion
  46.0 1.1 %copy.18 = f32[1,1,4,16,2048]{4,3,2,1,0:T(8,128)} copy(f32[1,1,4,16,2048]{4,2,3,1,0:T(4,128)S(1)} %select_bitcast_fusion) | data formatting | bytes 1048576 | tf_op jit(solution)/shard_map/broadcast_in_dim | solution.py:86
  (23 shorter events, 0.3 us)
Async XLA Ops:
  0.0 21.4 %copy-start = (bf16[1,1,16,128,128]{4,3,2,1,0:T(8,128)(2,1)S(1)}, bf16[1,1,16,128,128]{4,3,2,1,0:T(8,128)(2,1)}, u32[]{:S(2)}) copy-start(bf16[1,1,16,128,128]{4,3,2,1,0:T(8,128)(2,1)} %param.20) | copy-start | bytes 1572868
  1.5 9.5 %collective-permute-start = (f32[4,16,1]{2,0,1:T(4,128)S(1)}, f32[4,16,1]{2,0,1:T(4,128)S(1)}, u32[]{:S(2)}, u32[]{:S(2)}) collective-permute-start(f32[4,16,1]{2,0,1:T(4,128)S(1)} %get-tuple-element.35), channel_id=1, source_target_pairs={{0,1},{1,2},{2,3},{3,4},{4,5},{5,6},{6,7},{7,0},{8,9},{9,10},{10,1... | collective-permute-start | bytes 776 | tf_op jit(solution)/shard_map/ppermute | solution.py:17
  4.5 6.5 %collective-permute-start.1 = (f32[4,16,1]{2,0,1:T(4,128)S(1)}, f32[4,16,1]{2,0,1:T(4,128)S(1)}, u32[]{:S(2)}, u32[]{:S(2)}) collective-permute-start(f32[4,16,1]{2,0,1:T(4,128)S(1)} %get-tuple-element.36), channel_id=1, source_target_pairs={{1,0},{2,1},{3,2},{4,3},{5,4},{6,5},{7,6},{0,7},{9,8},{10,9},{11,1... | collective-permute-start | bytes 776 | tf_op jit(solution)/shard_map/ppermute | solution.py:19
  7.6 0.7 %copy-start.4 = (f32[2,4]{1,0:T(2,128)S(1)}, f32[2,4]{1,0:T(2,128)}, u32[]{:S(2)}) copy-start(f32[2,4]{1,0:T(2,128)} %param.16) | copy-start | bytes 100
  8.3 0.7 %copy-start.7 = (s32[1,1,16]{2,1,0:T(1,128)S(1)}, s32[1,1,16]{2,1,0:T(1,128)}, u32[]{:S(2)}) copy-start(s32[1,1,16]{2,1,0:T(1,128)} %param.17) | copy-start | bytes 196
  9.0 0.7 %copy-start.5 = (s32[1,1,16]{2,1,0:T(1,128)S(1)}, s32[1,1,16]{2,1,0:T(1,128)}, u32[]{:S(2)}) copy-start(s32[1,1,16]{2,1,0:T(1,128)} %param.18) | copy-start | bytes 196
  9.6 0.7 %copy-start.6 = (s32[1,1,16]{2,1,0:T(1,128)S(1)}, s32[1,1,16]{2,1,0:T(1,128)}, u32[]{:S(2)}) copy-start(s32[1,1,16]{2,1,0:T(1,128)} %param.19) | copy-start | bytes 196
  10.3 0.7 %copy-start.3 = (f32[2,4,16]{2,1,0:T(4,128)S(1)}, f32[2,4,16]{2,1,0:T(4,128)}, u32[]{:S(2)}) copy-start(f32[2,4,16]{2,1,0:T(4,128)} %param.14) | copy-start | bytes 1540
  11.8 6.6 %collective-permute-start.2 = (f32[4,16,1]{2,0,1:T(4,128)S(1)}, f32[4,16,1]{2,0,1:T(4,128)S(1)}, u32[]{:S(2)}, u32[]{:S(2)}) collective-permute-start(f32[4,16,1]{2,0,1:T(4,128)S(1)} %get-tuple-element.33), channel_id=1, source_target_pairs={{0,1},{1,2},{2,3},{3,4},{4,5},{5,6},{6,7},{7,0},{8,9},{9,10},{10,1... | collective-permute-start | bytes 776 | tf_op jit(solution)/shard_map/ppermute | solution.py:17
  11.8 6.6 %collective-permute-start.3 = (f32[4,16,1]{2,0,1:T(4,128)S(1)}, f32[4,16,1]{2,0,1:T(4,128)S(1)}, u32[]{:S(2)}, u32[]{:S(2)}) collective-permute-start(f32[4,16,1]{2,0,1:T(4,128)S(1)} %get-tuple-element.34), channel_id=1, source_target_pairs={{1,0},{2,1},{3,2},{4,3},{5,4},{6,5},{7,6},{0,7},{9,8},{10,9},{11,1... | collective-permute-start | bytes 776 | tf_op jit(solution)/shard_map/ppermute | solution.py:19
  16.5 2.5 %copy-start.2 = (f32[2,16,16]{2,1,0:T(8,128)S(1)}, f32[2,16,16]{2,1,0:T(8,128)}, u32[]{:S(2)}) copy-start(f32[2,16,16]{2,1,0:T(8,128)} %param.15) | copy-start | bytes 6148
  22.0 7.7 %collective-permute-start.4 = (f32[4,2048]{1,0:T(4,128)S(1)}, f32[4,2048]{1,0:T(4,128)S(1)}, u32[]{:S(2)}, u32[]{:S(2)}) collective-permute-start(f32[4,2048]{1,0:T(4,128)S(1)} %bitcast.117), channel_id=1, source_target_pairs={{0,5},{1,6},{2,7},{3,0},{4,1},{5,2},{6,3},{7,4},{8,13},{9,14},{10,... | collective-permute-start | bytes 98312 | tf_op jit(solution)/shard_map/ppermute | solution.py:29
  23.7 7.6 %collective-permute-start.5 = (f32[4,2048]{1,0:T(4,128)S(1)}, f32[4,2048]{1,0:T(4,128)S(1)}, u32[]{:S(2)}, u32[]{:S(2)}) collective-permute-start(f32[4,2048]{1,0:T(4,128)S(1)} %bitcast.115), channel_id=1, source_target_pairs={{0,6},{1,7},{2,0},{3,1},{4,2},{5,3},{6,4},{7,5},{8,14},{9,15},{10,... | collective-permute-start | bytes 98312 | tf_op jit(solution)/shard_map/ppermute | solution.py:29
  25.1 6.2 %collective-permute-start.6 = (f32[4,2048]{1,0:T(4,128)S(1)}, f32[4,2048]{1,0:T(4,128)S(1)}, u32[]{:S(2)}, u32[]{:S(2)}) collective-permute-start(f32[4,2048]{1,0:T(4,128)S(1)} %bitcast.116), channel_id=1, source_target_pairs={{0,7},{1,0},{2,1},{3,2},{4,3},{5,4},{6,5},{7,6},{8,15},{9,8},{10,9... | collective-permute-start | bytes 98312 | tf_op jit(solution)/shard_map/ppermute | solution.py:29
  27.0 6.7 %collective-permute-start.7 = (f32[4,2048]{1,0:T(4,128)S(1)}, f32[4,2048]{1,0:T(4,128)S(1)}, u32[]{:S(2)}, u32[]{:S(2)}) collective-permute-start(f32[4,2048]{1,0:T(4,128)S(1)} %bitcast.118), channel_id=1, source_target_pairs={{0,1},{1,2},{2,3},{3,4},{4,5},{5,6},{6,7},{7,0},{8,9},{9,10},{10,1... | collective-permute-start | bytes 98312 | tf_op jit(solution)/shard_map/ppermute | solution.py:29
  27.6 6.0 %collective-permute-start.8 = (f32[4,2048]{1,0:T(4,128)S(1)}, f32[4,2048]{1,0:T(4,128)S(1)}, u32[]{:S(2)}, u32[]{:S(2)}) collective-permute-start(f32[4,2048]{1,0:T(4,128)S(1)} %bitcast.119), channel_id=1, source_target_pairs={{0,2},{1,3},{2,4},{3,5},{4,6},{5,7},{6,0},{7,1},{8,10},{9,11},{10,... | collective-permute-start | bytes 98312 | tf_op jit(solution)/shard_map/ppermute | solution.py:29
  29.6 1.5 %copy-start.1 = (s32[1,2048]{1,0:T(1,128)S(1)}, s32[1,2048]{1,0:T(1,128)}, u32[]{:S(2)}) copy-start(s32[1,2048]{1,0:T(1,128)} %param.21) | copy-start | bytes 24580
  29.7 5.8 %collective-permute-start.9 = (f32[4,2048]{1,0:T(4,128)S(1)}, f32[4,2048]{1,0:T(4,128)S(1)}, u32[]{:S(2)}, u32[]{:S(2)}) collective-permute-start(f32[4,2048]{1,0:T(4,128)S(1)} %bitcast.120), channel_id=1, source_target_pairs={{0,3},{1,4},{2,5},{3,6},{4,7},{5,0},{6,1},{7,2},{8,11},{9,12},{10,... | collective-permute-start | bytes 98312 | tf_op jit(solution)/shard_map/ppermute | solution.py:29
where the time goes:
time: 47.4 us; the launch traced here: 47.1 us
  starting transfers between devices  19.9 us (42%)
  blocking collectives  10.3 us (22%)
  local copies, waits for them, and re-layouts  6.88 us (15%)
  waiting for transfers between devices  6.07 us (13%)
  other arithmetic  2.36 us (5%)
  matrix products  1.45 us (3%)
    psum x1, blocking collectives, local(): received = lax.psum(received, 'comp')  10.3 us
    ppermute x6, starting transfers between devices, passed_along(): return lax.ppermute(value, axis, pairs)  9.11 us
    ppermute x2, starting transfers between devices, extended(): lax.ppermute(head, axis, [((i + 1) % count, i) for i in range(count)])  7.81 us
    unnamed x26, local copies, waits for them, and re-layouts  4.92 us
    ppermute x6, waiting for transfers between devices, passed_along(): return lax.ppermute(value, axis, pairs)  4.18 us
    ppermute x2, starting transfers between devices, extended(): lax.ppermute(tail, axis, [(i, (i + 1) % count) for i in range(count)])  3.02 us
    ppermute x2, waiting for transfers between devices, extended(): lax.ppermute(tail, axis, [(i, (i + 1) % count) for i in range(count)])  1.88 us
    add x2, other arithmetic, local(): fields + rates * (padded[:, :, :-2] + padded[:, :, 2:] - 2.0 * fields)  1.28 us
  transfers between devices with their start and end apart: 10, of which 3 were waited for; matrix products, arithmetic and copies ran while one was open for 0% of the time, Pallas kernels for 0%

commit v1 on v0

--- a/solution.py
+++ b/solution.py
@@ -78,7 +78,7 @@
     for offset in range(-REACH, REACH + 1):
         if offset != 0:
             received = received + passed_along(buffers[REACH + offset], "tile", offset)
-    received = lax.psum(received, "comp")
+    received = jnp.sum(lax.all_gather(received, "comp"), axis=0)
     land = ocean_mask[0].astype(jnp.float32)
     atmosphere = mixed.at[:, -1].add(-0.5 * surface)
     ocean = mixed.at[:, 0].add(land[None, :] * received)

time: 47.4 us -> 42.6 us (0.90)
  blocking collectives: 10.3 us -> 5.42 us
    psum x1 -> x0, blocking collectives: 10.3 us -> none  [local(): received = lax.psum(received, 'comp')]
    all_gather x0 -> x1, blocking collectives: none -> 5.42 us  [local(): received = jnp.sum(lax.all_gather(received, 'comp'), axis=0)]
  transfers between devices with their start and end apart: 10 -> 10, of which waited for: 3 -> 3; matrix products, arithmetic and copies ran while one was open for 0% -> 1% of each run, Pallas kernels for 0% -> 0%
where the time goes in v1:
time: 42.6 us; the launch traced here: 42.3 us
  starting transfers between devices  19.9 us (47%)
  local copies, waits for them, and re-layouts  6.88 us (16%)
  waiting for transfers between devices  6.07 us (14%)
  blocking collectives  5.42 us (13%)
  other arithmetic  2.38 us (6%)
  matrix products  1.45 us (3%)
    ppermute x6, starting transfers between devices, passed_along(): return lax.ppermute(value, axis, pairs)  9.11 us
    ppermute x2, starting transfers between devices, extended(): lax.ppermute(head, axis, [((i + 1) % count, i) for i in range(count)])  7.81 us
    all_gather x1, blocking collectives, local(): received = jnp.sum(lax.all_gather(received, 'comp'), axis=0)  5.42 us
    unnamed x26, local copies, waits for them, and re-layouts  4.92 us
    ppermute x6, waiting for transfers between devices, passed_along(): return lax.ppermute(value, axis, pairs)  4.18 us
    ppermute x2, starting transfers between devices, extended(): lax.ppermute(tail, axis, [(i, (i + 1) % count) for i in range(count)])  3.02 us
    ppermute x2, waiting for transfers between devices, extended(): lax.ppermute(tail, axis, [(i, (i + 1) % count) for i in range(count)])  1.88 us
    add x2, other arithmetic, local(): fields + rates * (padded[:, :, :-2] + padded[:, :, 2:] - 2.0 * fields)  1.28 us
  transfers between devices with their start and end apart: 10, of which 3 were waited for; matrix products, arithmetic and copies ran while one was open for 1% of the time, Pallas kernels for 0%

profile of v1, /device:TPU:0, one launch (start us, length us, event | category | flops | bytes accessed | tf_op | source)
XLA Modules:
  0.0 42.3 jit_solution(9136632991708031139)
XLA Ops:
  0.0 0.0 copy-start
  0.0 1.4 %copy.49 = f32[1,1,4,16,2048]{4,2,3,1,0:T(4,128)S(1)} copy(f32[1,1,4,16,2048]{4,3,2,1,0:T(8,128)} %param.13) | data formatting | bytes 1048576 | tf_op args[0]
  1.4 0.1 fusion.37
  1.5 3.0 %collective-permute-start = (f32[4,16,1]{2,0,1:T(4,128)S(1)}, f32[4,16,1]{2,0,1:T(4,128)S(1)}, u32[]{:S(2)}, u32[]{:S(2)}) collective-permute-start(f32[4,16,1]{2,0,1:T(4,128)S(1)} %get-tuple-element.35), channel_id=1, source_target_pairs={{0,1},{1,2},{2,3},{3,4},{4,5},{5,6},{6,7},{7,0},{8,9},{9,10},{10,1... | collective-permute-start | bytes 776 | tf_op jit(solution)/shard_map/ppermute | solution.py:17
  4.5 3.1 %collective-permute-start.1 = (f32[4,16,1]{2,0,1:T(4,128)S(1)}, f32[4,16,1]{2,0,1:T(4,128)S(1)}, u32[]{:S(2)}, u32[]{:S(2)}) collective-permute-start(f32[4,16,1]{2,0,1:T(4,128)S(1)} %get-tuple-element.36), channel_id=1, source_target_pairs={{1,0},{2,1},{3,2},{4,3},{5,4},{6,5},{7,6},{0,7},{9,8},{10,9},{11,1... | collective-permute-start | bytes 776 | tf_op jit(solution)/shard_map/ppermute | solution.py:19
  7.6 0.0 copy-start.4
  7.6 0.7 %copy-done.4 = f32[2,4]{1,0:T(2,128)S(1)} copy-done((f32[2,4]{1,0:T(2,128)S(1)}, f32[2,4]{1,0:T(2,128)}, u32[]{:S(2)}) %copy-start.4) | copy-done | bytes 56
  8.3 0.0 copy-start.7
  8.3 0.6 %copy-done.7 = s32[1,1,16]{2,1,0:T(1,128)S(1)} copy-done((s32[1,1,16]{2,1,0:T(1,128)S(1)}, s32[1,1,16]{2,1,0:T(1,128)}, u32[]{:S(2)}) %copy-start.7) | copy-done | bytes 88
  9.0 0.0 copy-start.5
  9.0 0.7 %copy-done.5 = s32[1,1,16]{2,1,0:T(1,128)S(1)} copy-done((s32[1,1,16]{2,1,0:T(1,128)S(1)}, s32[1,1,16]{2,1,0:T(1,128)}, u32[]{:S(2)}) %copy-start.5) | copy-done | bytes 88
  9.6 0.7 %copy-done.6 = s32[1,1,16]{2,1,0:T(1,128)S(1)} copy-done((s32[1,1,16]{2,1,0:T(1,128)S(1)}, s32[1,1,16]{2,1,0:T(1,128)}, u32[]{:S(2)}) %copy-start.6) | copy-done | bytes 88
  10.3 0.7 %copy-done.3 = f32[2,4,16]{2,1,0:T(4,128)S(1)} copy-done((f32[2,4,16]{2,1,0:T(4,128)S(1)}, f32[2,4,16]{2,1,0:T(4,128)}, u32[]{:S(2)}) %copy-start.3) | copy-done | bytes 536
  11.0 0.1 copy.16
  11.1 0.0 collective-permute-done
  11.1 0.0 collective-permute-done.1
  11.1 0.6 %fusion.8 = f32[4,16,2048]{2,0,1:T(4,128)S(1)} fusion(f32[4,16,2048]{2,0,1:T(4,128)S(1)} %bitcast.120, f32[4,16,1]{2,0,1:T(4,128)S(1)} %collective-permute-done.1, f32[4,16,1]{2,0,1:T(4,128)S(1)} %collective-permute-done, f32[4,16]{0,1:T(8,128)S(1)} %copy.16), kind=kLoop, calls=%fused_computation.13 | loop fusion | flops 917504 | bytes 1049344 | tf_op jit(solution)/shard_map/add | solution.py:57
  11.7 0.1 fusion.36
  11.8 0.0 collective-permute-start.2
  11.8 4.7 %collective-permute-start.3 = (f32[4,16,1]{2,0,1:T(4,128)S(1)}, f32[4,16,1]{2,0,1:T(4,128)S(1)}, u32[]{:S(2)}, u32[]{:S(2)}) collective-permute-start(f32[4,16,1]{2,0,1:T(4,128)S(1)} %get-tuple-element.34), channel_id=1, source_target_pairs={{1,0},{2,1},{3,2},{4,3},{5,4},{6,5},{7,6},{0,7},{9,8},{10,9},{11,1... | collective-permute-start | bytes 776 | tf_op jit(solution)/shard_map/ppermute | solution.py:19
  16.5 1.9 %collective-permute-done.2 = f32[4,16,1]{2,0,1:T(4,128)S(1)} collective-permute-done((f32[4,16,1]{2,0,1:T(4,128)S(1)}, f32[4,16,1]{2,0,1:T(4,128)S(1)}, u32[]{:S(2)}, u32[]{:S(2)}) %collective-permute-start.2) | collective-permute-done | bytes 288 | tf_op jit(solution)/shard_map/ppermute | solution.py:17
  18.4 0.0 collective-permute-done.3
  18.4 0.6 %fusion.4 = f32[4,16,2048]{2,0,1:T(4,128)S(1)} fusion(f32[4,16,2048]{2,0,1:T(4,128)S(1)} %fusion.8, f32[4,16,1]{2,0,1:T(4,128)S(1)} %collective-permute-done.3, f32[4,16,1]{2,0,1:T(4,128)S(1)} %collective-permute-done.2, f32[4,16]{0,1:T(8,128)S(1)} %copy.16), kind=kLoop, calls=%fused_computation.7 | loop fusion | flops 917504 | bytes 1049344 | tf_op jit(solution)/shard_map/add | solution.py:57
  19.1 0.0 copy-done.2
  19.1 0.9 %fusion.11 = f32[4,2048,16]{1,2,0:T(8,128)S(1)} fusion(f32[4,16,2048]{2,0,1:T(4,128)S(1)} %fusion.4, f32[2,16,16]{2,1,0:T(8,128)S(1)} %copy-done.2, s32[]{:T(128)S(6)} %select_n.39), kind=kOutput, calls=%fused_computation.18 | convolution fusion | flops 25165824 | bytes 1056772 | tf_op jit(solution)/shard_map/lm,kmz->klz/dot_general | solution.py:58
  20.0 0.7 %bitcast_add_fusion = f32[4,16,2048]{2,0,1:T(4,128)S(1)} fusion(f32[4,2048,16]{1,2,0:T(8,128)S(1)} %fusion.11, f32[4,16,2048]{2,0,1:T(4,128)S(1)} %fusion.8, f32[4,16,1]{2,0,1:T(4,128)S(1)} %collective-permute-done.3, f32[4,16,1]{2,0,1:T(4,128)S(1)} %collective-permute-done.2, f32[4,16]{0,1:T(8,128)S(1)} %copy.16), kind=kLoop, calls=%fused_computation.17 | loop fusion | flops 1048576 | bytes 1573632 | tf_op jit(solution)/shard_map/add | solution.py:58
  20.7 0.1 fusion.23
  20.8 0.6 %gather_fusion = bf16[16,4,128]{2,1,0:T(4,128)(2,1)S(1)} fusion(bf16[4,16,128]{2,0,1:T(4,128)(2,1)S(1)} %copy.19, s32[1024]{0:T(1024)S(1)} %pad_clamp_fusion), kind=kCustom, calls=%fused_computation | custom fusion | bytes 32832 | tf_op jit(solution)/shard_map/gather | solution.py:62
  21.4 0.0 copy-done
  21.4 0.2 fusion.9
  21.6 0.3 fusion
  22.0 1.6 %collective-permute-start.4 = (f32[4,2048]{1,0:T(4,128)S(1)}, f32[4,2048]{1,0:T(4,128)S(1)}, u32[]{:S(2)}, u32[]{:S(2)}) collective-permute-start(f32[4,2048]{1,0:T(4,128)S(1)} %bitcast.123), channel_id=1, source_target_pairs={{0,5},{1,6},{2,7},{3,0},{4,1},{5,2},{6,3},{7,4},{8,13},{9,14},{10,... | collective-permute-start | bytes 98312 | tf_op jit(solution)/shard_map/ppermute | solution.py:29
  23.7 1.4 %collective-permute-start.5 = (f32[4,2048]{1,0:T(4,128)S(1)}, f32[4,2048]{1,0:T(4,128)S(1)}, u32[]{:S(2)}, u32[]{:S(2)}) collective-permute-start(f32[4,2048]{1,0:T(4,128)S(1)} %bitcast.121), channel_id=1, source_target_pairs={{0,6},{1,7},{2,0},{3,1},{4,2},{5,3},{6,4},{7,5},{8,14},{9,15},{10,... | collective-permute-start | bytes 98312 | tf_op jit(solution)/shard_map/ppermute | solution.py:29
  25.1 1.9 %collective-permute-start.6 = (f32[4,2048]{1,0:T(4,128)S(1)}, f32[4,2048]{1,0:T(4,128)S(1)}, u32[]{:S(2)}, u32[]{:S(2)}) collective-permute-start(f32[4,2048]{1,0:T(4,128)S(1)} %bitcast.122), channel_id=1, source_target_pairs={{0,7},{1,0},{2,1},{3,2},{4,3},{5,4},{6,5},{7,6},{8,15},{9,8},{10,9... | collective-permute-start | bytes 98312 | tf_op jit(solution)/shard_map/ppermute | solution.py:29
  27.0 0.6 %collective-permute-start.7 = (f32[4,2048]{1,0:T(4,128)S(1)}, f32[4,2048]{1,0:T(4,128)S(1)}, u32[]{:S(2)}, u32[]{:S(2)}) collective-permute-start(f32[4,2048]{1,0:T(4,128)S(1)} %bitcast.124), channel_id=1, source_target_pairs={{0,1},{1,2},{2,3},{3,4},{4,5},{5,6},{6,7},{7,0},{8,9},{9,10},{10,1... | collective-permute-start | bytes 98312 | tf_op jit(solution)/shard_map/ppermute | solution.py:29
  27.6 2.1 %collective-permute-start.8 = (f32[4,2048]{1,0:T(4,128)S(1)}, f32[4,2048]{1,0:T(4,128)S(1)}, u32[]{:S(2)}, u32[]{:S(2)}) collective-permute-start(f32[4,2048]{1,0:T(4,128)S(1)} %bitcast.125), channel_id=1, source_target_pairs={{0,2},{1,3},{2,4},{3,5},{4,6},{5,7},{6,0},{7,1},{8,10},{9,11},{10,... | collective-permute-start | bytes 98312 | tf_op jit(solution)/shard_map/ppermute | solution.py:29
  29.7 0.0 collective-permute-done.4
  29.7 1.5 %collective-permute-start.9 = (f32[4,2048]{1,0:T(4,128)S(1)}, f32[4,2048]{1,0:T(4,128)S(1)}, u32[]{:S(2)}, u32[]{:S(2)}) collective-permute-start(f32[4,2048]{1,0:T(4,128)S(1)} %bitcast.126), channel_id=1, source_target_pairs={{0,3},{1,4},{2,5},{3,6},{4,7},{5,0},{6,1},{7,2},{8,11},{9,12},{10,... | collective-permute-start | bytes 98312 | tf_op jit(solution)/shard_map/ppermute | solution.py:29
  31.2 0.0 copy-done.1
  31.3 0.0 collective-permute-done.5
  31.3 0.0 collective-permute-done.6
  31.3 2.3 %collective-permute-done.7 = f32[4,2048]{1,0:T(4,128)S(1)} collective-permute-done((f32[4,2048]{1,0:T(4,128)S(1)}, f32[4,2048]{1,0:T(4,128)S(1)}, u32[]{:S(2)}, u32[]{:S(2)}) %collective-permute-start.7) | collective-permute-done | bytes 32800 | tf_op jit(solution)/shard_map/ppermute | solution.py:29
  33.6 0.0 collective-permute-done.8
  33.6 1.8 %collective-permute-done.9 = f32[4,2048]{1,0:T(4,128)S(1)} collective-permute-done((f32[4,2048]{1,0:T(4,128)S(1)}, f32[4,2048]{1,0:T(4,128)S(1)}, u32[]{:S(2)}, u32[]{:S(2)}) %collective-permute-start.9) | collective-permute-done | bytes 32800 | tf_op jit(solution)/shard_map/ppermute | solution.py:29
  35.5 5.4 %all-gather.1 = f32[4,4,2048]{2,1,0:T(4,128)S(1)} all-gather(f32[1,4,2048]{2,1,0:T(4,128)S(1)} %fusion.20), channel_id=2, replica_groups=mesh['comp'=4,'tile'=8] {'comp'}, dimensions={0}, use_global_device_ids=true | all-gather | bytes 163840 | tf_op jit(solution)/shard_map/all_gather | solution.py:81
  41.0 0.1 add_dynamic-update-slice_fusion
  41.1 0.1 select_bitcast_fusion
  41.2 1.1 %copy.21 = f32[1,1,4,16,2048]{4,3,2,1,0:T(8,128)} copy(f32[1,1,4,16,2048]{4,2,3,1,0:T(4,128)S(1)} %select_bitcast_fusion) | data formatting | bytes 1048576 | tf_op jit(solution)/shard_map/broadcast_in_dim | solution.py:86
  (24 shorter events, 0.3 us)
Async XLA Ops:
  0.0 21.4 %copy-start = (bf16[1,1,16,128,128]{4,3,2,1,0:T(8,128)(2,1)S(1)}, bf16[1,1,16,128,128]{4,3,2,1,0:T(8,128)(2,1)}, u32[]{:S(2)}) copy-start(bf16[1,1,16,128,128]{4,3,2,1,0:T(8,128)(2,1)} %param.20) | copy-start | bytes 1572868
  1.5 9.5 %collective-permute-start = (f32[4,16,1]{2,0,1:T(4,128)S(1)}, f32[4,16,1]{2,0,1:T(4,128)S(1)}, u32[]{:S(2)}, u32[]{:S(2)}) collective-permute-start(f32[4,16,1]{2,0,1:T(4,128)S(1)} %get-tuple-element.35), channel_id=1, source_target_pairs={{0,1},{1,2},{2,3},{3,4},{4,5},{5,6},{6,7},{7,0},{8,9},{9,10},{10,1... | collective-permute-start | bytes 776 | tf_op jit(solution)/shard_map/ppermute | solution.py:17
  4.5 6.5 %collective-permute-start.1 = (f32[4,16,1]{2,0,1:T(4,128)S(1)}, f32[4,16,1]{2,0,1:T(4,128)S(1)}, u32[]{:S(2)}, u32[]{:S(2)}) collective-permute-start(f32[4,16,1]{2,0,1:T(4,128)S(1)} %get-tuple-element.36), channel_id=1, source_target_pairs={{1,0},{2,1},{3,2},{4,3},{5,4},{6,5},{7,6},{0,7},{9,8},{10,9},{11,1... | collective-permute-start | bytes 776 | tf_op jit(solution)/shard_map/ppermute | solution.py:19
  7.6 0.7 %copy-start.4 = (f32[2,4]{1,0:T(2,128)S(1)}, f32[2,4]{1,0:T(2,128)}, u32[]{:S(2)}) copy-start(f32[2,4]{1,0:T(2,128)} %param.16) | copy-start | bytes 100
  8.3 0.7 %copy-start.7 = (s32[1,1,16]{2,1,0:T(1,128)S(1)}, s32[1,1,16]{2,1,0:T(1,128)}, u32[]{:S(2)}) copy-start(s32[1,1,16]{2,1,0:T(1,128)} %param.17) | copy-start | bytes 196
  9.0 0.7 %copy-start.5 = (s32[1,1,16]{2,1,0:T(1,128)S(1)}, s32[1,1,16]{2,1,0:T(1,128)}, u32[]{:S(2)}) copy-start(s32[1,1,16]{2,1,0:T(1,128)} %param.18) | copy-start | bytes 196
  9.6 0.7 %copy-start.6 = (s32[1,1,16]{2,1,0:T(1,128)S(1)}, s32[1,1,16]{2,1,0:T(1,128)}, u32[]{:S(2)}) copy-start(s32[1,1,16]{2,1,0:T(1,128)} %param.19) | copy-start | bytes 196
  10.3 0.7 %copy-start.3 = (f32[2,4,16]{2,1,0:T(4,128)S(1)}, f32[2,4,16]{2,1,0:T(4,128)}, u32[]{:S(2)}) copy-start(f32[2,4,16]{2,1,0:T(4,128)} %param.14) | copy-start | bytes 1540
  11.8 6.6 %collective-permute-start.2 = (f32[4,16,1]{2,0,1:T(4,128)S(1)}, f32[4,16,1]{2,0,1:T(4,128)S(1)}, u32[]{:S(2)}, u32[]{:S(2)}) collective-permute-start(f32[4,16,1]{2,0,1:T(4,128)S(1)} %get-tuple-element.33), channel_id=1, source_target_pairs={{0,1},{1,2},{2,3},{3,4},{4,5},{5,6},{6,7},{7,0},{8,9},{9,10},{10,1... | collective-permute-start | bytes 776 | tf_op jit(solution)/shard_map/ppermute | solution.py:17
  11.8 6.6 %collective-permute-start.3 = (f32[4,16,1]{2,0,1:T(4,128)S(1)}, f32[4,16,1]{2,0,1:T(4,128)S(1)}, u32[]{:S(2)}, u32[]{:S(2)}) collective-permute-start(f32[4,16,1]{2,0,1:T(4,128)S(1)} %get-tuple-element.34), channel_id=1, source_target_pairs={{1,0},{2,1},{3,2},{4,3},{5,4},{6,5},{7,6},{0,7},{9,8},{10,9},{11,1... | collective-permute-start | bytes 776 | tf_op jit(solution)/shard_map/ppermute | solution.py:19
  16.5 2.5 %copy-start.2 = (f32[2,16,16]{2,1,0:T(8,128)S(1)}, f32[2,16,16]{2,1,0:T(8,128)}, u32[]{:S(2)}) copy-start(f32[2,16,16]{2,1,0:T(8,128)} %param.15) | copy-start | bytes 6148
  22.0 7.7 %collective-permute-start.4 = (f32[4,2048]{1,0:T(4,128)S(1)}, f32[4,2048]{1,0:T(4,128)S(1)}, u32[]{:S(2)}, u32[]{:S(2)}) collective-permute-start(f32[4,2048]{1,0:T(4,128)S(1)} %bitcast.123), channel_id=1, source_target_pairs={{0,5},{1,6},{2,7},{3,0},{4,1},{5,2},{6,3},{7,4},{8,13},{9,14},{10,... | collective-permute-start | bytes 98312 | tf_op jit(solution)/shard_map/ppermute | solution.py:29
  23.7 7.6 %collective-permute-start.5 = (f32[4,2048]{1,0:T(4,128)S(1)}, f32[4,2048]{1,0:T(4,128)S(1)}, u32[]{:S(2)}, u32[]{:S(2)}) collective-permute-start(f32[4,2048]{1,0:T(4,128)S(1)} %bitcast.121), channel_id=1, source_target_pairs={{0,6},{1,7},{2,0},{3,1},{4,2},{5,3},{6,4},{7,5},{8,14},{9,15},{10,... | collective-permute-start | bytes 98312 | tf_op jit(solution)/shard_map/ppermute | solution.py:29
  25.1 6.2 %collective-permute-start.6 = (f32[4,2048]{1,0:T(4,128)S(1)}, f32[4,2048]{1,0:T(4,128)S(1)}, u32[]{:S(2)}, u32[]{:S(2)}) collective-permute-start(f32[4,2048]{1,0:T(4,128)S(1)} %bitcast.122), channel_id=1, source_target_pairs={{0,7},{1,0},{2,1},{3,2},{4,3},{5,4},{6,5},{7,6},{8,15},{9,8},{10,9... | collective-permute-start | bytes 98312 | tf_op jit(solution)/shard_map/ppermute | solution.py:29
  27.0 6.7 %collective-permute-start.7 = (f32[4,2048]{1,0:T(4,128)S(1)}, f32[4,2048]{1,0:T(4,128)S(1)}, u32[]{:S(2)}, u32[]{:S(2)}) collective-permute-start(f32[4,2048]{1,0:T(4,128)S(1)} %bitcast.124), channel_id=1, source_target_pairs={{0,1},{1,2},{2,3},{3,4},{4,5},{5,6},{6,7},{7,0},{8,9},{9,10},{10,1... | collective-permute-start | bytes 98312 | tf_op jit(solution)/shard_map/ppermute | solution.py:29
  27.6 6.0 %collective-permute-start.8 = (f32[4,2048]{1,0:T(4,128)S(1)}, f32[4,2048]{1,0:T(4,128)S(1)}, u32[]{:S(2)}, u32[]{:S(2)}) collective-permute-start(f32[4,2048]{1,0:T(4,128)S(1)} %bitcast.125), channel_id=1, source_target_pairs={{0,2},{1,3},{2,4},{3,5},{4,6},{5,7},{6,0},{7,1},{8,10},{9,11},{10,... | collective-permute-start | bytes 98312 | tf_op jit(solution)/shard_map/ppermute | solution.py:29
  29.6 1.5 %copy-start.1 = (s32[1,2048]{1,0:T(1,128)S(1)}, s32[1,2048]{1,0:T(1,128)}, u32[]{:S(2)}) copy-start(s32[1,2048]{1,0:T(1,128)} %param.21) | copy-start | bytes 24580
  29.7 5.8 %collective-permute-start.9 = (f32[4,2048]{1,0:T(4,128)S(1)}, f32[4,2048]{1,0:T(4,128)S(1)}, u32[]{:S(2)}, u32[]{:S(2)}) collective-permute-start(f32[4,2048]{1,0:T(4,128)S(1)} %bitcast.126), channel_id=1, source_target_pairs={{0,3},{1,4},{2,5},{3,6},{4,7},{5,0},{6,1},{7,2},{8,11},{9,12},{10,... | collective-permute-start | bytes 98312 | tf_op jit(solution)/shard_map/ppermute | solution.py:29
